TPU v7x, 32 devices: a whole 2x2x4 slice. The times are simulated.
32 devices in a mesh: row: 4 (over x, core), col: 8 (over z, y).
Axes of the slice: x: 2, y: 2, z: 4, core: 2. Of those that a mesh axis runs over, the one named last changes fastest.
Arguments:
- solution: float32 [16384, 128], P(('row', 'col')), may hold values from -6 to 6
- right_side: float32 [16384, 128], P(('row', 'col')), may hold values from -6 to 6
- block_values: bfloat16 [128, 32, 128, 128], P('row', 'col'), may hold values from -0.09375 to 0.09375
- block_columns: int32 [128, 32], P('row', 'col'), may hold values from 0 to 127, as said below
- row_order: int32 [16384], P(('row', 'col')), may hold values from 0 to 16383, as said below
- tri_inverses: bfloat16 [8192, 12288], P(('row', 'col')), may hold values from -1 to 2
- lower_updates: bfloat16 [4096, 8192], P(None, ('row', 'col')), may hold values from -0.09375 to 0.09375
- upper_updates: bfloat16 [8192, 4096], P(('row', 'col')), may hold values from -0.09375 to 0.09375
- update_rows: int32 [1, 8192], replicated, may hold values from 0 to 8191, as said below
Outputs:
- refined: float32 [16384, 128], P(('row', 'col'))
- residual: float32 [16384, 128], P(('row', 'col'))
Inputs may be any that keep to these rules, and one draw needn't show every extreme that they name: `block_columns`: for block row i and slot s, the named block b satisfies (b // 4) % (8) == s // 4. `row_order`: each aligned block of 512 entries is a permutation of that block's own positions. `update_rows`: in row k, each aligned block of 2^k * 4096 entries holds distinct values below 2^(k+1) * 4096.
All inputs are finite; a program needn't handle non-finite values.
Results may differ from a plain program's by a relative error of at most 0.02.
Values may be sent and summed in bfloat16 or wider, within the bound.
No kernel may reach another device: no remote copies, remote signals or barrier semaphores. Data moves between devices by JAX's collectives and lax.ppermute only.
A program may use at most 128 MiB of HBM per device.

v0:
```python
import jax
import jax.numpy as jnp
from jax import lax
from jax.sharding import PartitionSpec as P


def from_partner(block, axis, distance):
    count = lax.axis_size(axis)
    route = []
    for low in range(count):
        high = low | 1 << distance
        if high != low and high < count:
            route += [(low, high), (high, low)]
    return lax.ppermute(block, axis, route)


def column_sum(values):
    return lax.psum_scatter(values, "col", scatter_dimension=0, tiled=True)


def column_gather(values):
    return lax.all_gather(values, "col", axis=0, tiled=True)


def partner_values(values, bit_index):
    return from_partner(values, "row", bit_index)


def partner_totals(values, bit_index):
    return from_partner(values.astype(jnp.bfloat16), "row", bit_index).astype(values.dtype)


def join_rows(values, bit_count):
    position = lax.axis_index("row")
    for bit_index in range(bit_count):
        partner = partner_values(values, bit_index)
        raised = position >> bit_index & 1 == 1
        values = jnp.where(
            raised, jnp.concatenate([partner, values], 0), jnp.concatenate([values, partner], 0)
        )
    return values


def halve_rows(values, bit_count):
    position = lax.axis_index("row")
    for bit_index in reversed(range(bit_count)):
        middle = values.shape[0] // 2
        raised = position >> bit_index & 1 == 1
        retained = jnp.where(raised, values[middle:], values[:middle])
        outgoing = jnp.where(raised, values[:middle], values[middle:])
        values = retained + partner_totals(outgoing, bit_index)
    return values


def front_gather(values, bit_count):
    return join_rows(column_gather(values), bit_count)


def front_reduce(targets, partials, bit_count, seg_rows):
    col_count = lax.axis_size("col")
    group_rows = 2**bit_count
    total_rows = group_rows * col_count * seg_rows
    zeros_sum = jnp.zeros((total_rows, partials.shape[1]), jnp.float32)
    owner_row = targets // (col_count * seg_rows)
    owner_col = targets // seg_rows % col_count
    placed = (owner_col * group_rows + owner_row) * seg_rows + targets % seg_rows
    summed = column_sum(zeros_sum.at[placed].add(partials))
    return halve_rows(summed.reshape(group_rows, seg_rows, -1), bit_count)[0]


def triangle_rows(tri_panel, full_vector, first_row, strict_lower):
    row_ids = first_row + lax.broadcasted_iota(jnp.int32, tri_panel.shape, 0)
    col_ids = lax.broadcasted_iota(jnp.int32, tri_panel.shape, 1)
    keep_mask = col_ids < row_ids if strict_lower else col_ids >= row_ids
    masked = jnp.where(keep_mask, tri_panel, jnp.zeros_like(tri_panel))
    return jnp.dot(masked, full_vector, preferred_element_type=jnp.float32)


def on_device(
    solution,
    right_side,
    block_values,
    block_columns,
    row_order,
    tri_inverses,
    lower_updates,
    upper_updates,
    update_rows,
):
    row_count = lax.axis_size("row")
    col_count = lax.axis_size("col")
    levels_count = row_count.bit_length() - 1
    per_device = solution.shape[0]
    seg_rows = per_device // levels_count
    block_size = block_values.shape[2]
    per_block = per_device // block_size
    row_index = lax.axis_index("row")
    col_index = lax.axis_index("col")
    gathered = lax.all_gather(solution.astype(jnp.bfloat16), "row", axis=0, tiled=True).astype(
        solution.dtype
    )
    local_block = block_columns // (per_block * col_count) * per_block + block_columns % per_block
    solution_blocks = gathered.reshape(row_count * per_block, block_size, -1)
    picked = solution_blocks[local_block]
    applied = jnp.einsum(
        "iskl,isln->ikn", block_values.astype(jnp.float32), picked, precision=lax.Precision.HIGHEST
    )
    product = column_sum(applied.reshape(-1, applied.shape[-1]))
    residual = right_side - product
    device_index = row_index * col_count + col_index
    local_order = row_order - device_index * per_device
    permuted = residual[local_order]
    stacked = permuted.reshape(levels_count, seg_rows, -1)
    sep_bottom = 2 * col_count * seg_rows
    lowered = []
    targets_all = []
    first_rows = []
    incoming = None
    for depth_k in range(levels_count):
        groups = 2 ** (depth_k + 1)
        span_rows = sep_bottom * 2**depth_k
        offset_col = sep_bottom * (2**depth_k - 1)
        first_row = (row_index % groups * col_count + col_index) * seg_rows
        first_rows.append(first_row)
        current = stacked[depth_k]
        if depth_k > 0:
            current = current - incoming
        rounded = current.astype(jnp.bfloat16)
        front_full = front_gather(rounded, depth_k + 1)
        tri_panel = tri_inverses[:, offset_col : offset_col + span_rows]
        solved_rows = triangle_rows(tri_panel, front_full, first_row, True) + rounded.astype(
            jnp.float32
        )
        lower_rows = solved_rows.astype(jnp.bfloat16)
        lowered.append(lower_rows)
        if depth_k + 1 < levels_count:
            front_idx = row_index // groups
            chosen = lax.dynamic_slice_in_dim(
                update_rows[depth_k], front_idx * span_rows, span_rows
            )
            targets_all.append(chosen)
            partials = jnp.dot(
                lower_updates[offset_col : offset_col + span_rows],
                lower_rows,
                preferred_element_type=jnp.float32,
            )
            incoming = front_reduce(chosen, partials, depth_k + 2, seg_rows)
    corrections = [None] * levels_count
    parent_rows = None
    for depth_k in reversed(range(levels_count)):
        span_rows = sep_bottom * 2**depth_k
        offset_col = sep_bottom * (2**depth_k - 1)
        reduced = lowered[depth_k].astype(jnp.float32)
        if depth_k + 1 < levels_count:
            parent_full = front_gather(parent_rows, depth_k + 2)
            picked_rows = parent_full[targets_all[depth_k]]
            reduced = reduced - jnp.dot(
                upper_updates[:, offset_col : offset_col + span_rows],
                picked_rows,
                preferred_element_type=jnp.float32,
            )
        rounded = reduced.astype(jnp.bfloat16)
        full_vector = front_gather(rounded, depth_k + 1)
        tri_panel = tri_inverses[:, offset_col : offset_col + span_rows]
        upper_rows = triangle_rows(tri_panel, full_vector, first_rows[depth_k], False)
        corrections[depth_k] = upper_rows
        parent_rows = upper_rows.astype(jnp.bfloat16)
    correction = jnp.concatenate(corrections, 0)
    return (solution + correction, residual)


def solution(mesh):
    in_specs = (
        P(("row", "col"), None),
        P(("row", "col"), None),
        P("row", "col", None, None),
        P("row", "col"),
        P(("row", "col")),
        P(("row", "col"), None),
        P(None, ("row", "col")),
        P(("row", "col"), None),
        P(),
    )
    out_specs = (P(("row", "col"), None), P(("row", "col"), None))
    return jax.shard_map(
        on_device, mesh=mesh, in_specs=in_specs, out_specs=out_specs, check_vma=False
    )
```

profile of v0, /device:TPU:0, one launch (start us, length us, event | category | flops | bytes accessed | tf_op | source)
XLA Modules:
  0.0 503.0 jit_solution(4245050510529039252)
XLA Ops:
  9.2 8.6 %all_gather.18 = bf16[2048,128]{1,0:T(8,128)(2,1)S(1)} all-gather(bf16[512,128]{1,0:T(8,128)(2,1)S(1)} %convert_element_type.47), channel_id=1, replica_groups=mesh['row'=4,'col'=8] {'row'}, dimensions={0}, use_global_device_ids=true | all-gather | bytes 655360 | tf_op jit(solution)/shard_map/all_gather | solution.py:99
  17.9 3.0 gather_fusion
  20.9 6.1 %fusion.83 = f32[32,128,128,1]{1,2,3,0:T(8,128)} fusion(bf16[32,4,128,128]{3,2,1,0:T(8,128)(2,1)} %param.11, bf16[32,4,128,128]{3,2,1,0:T(8,128)(2,1)} %bitcast.50), kind=kOutput, calls=%fused_computation.125 | convolution fusion | flops 536870912 | bytes 10485760 | tf_op jit(solution)/shard_map/iskl,isln->ikn/dot_general | solution.py:105
  27.7 68.6 %reduce-scatter.3.cloned.1.call-done = f32[512,128]{1,0:T(8,128)} async-done(((f32[4096,128]{1,0:T(8,128)}), f32[512,128]{1,0:T(8,128)}) %reduce-scatter.3.cloned.1.call-update) | async-done | bytes 262160 | tf_op jit(solution)/shard_map/reduce_scatter | solution.py:18
  98.4 31.3 %all_gather.19 = bf16[2048,128]{1,0:T(8,128)(2,1)S(1)} all-gather(bf16[256,128]{1,0:T(8,128)(2,1)S(1)} %slice.91), channel_id=1, replica_groups=mesh['row'=4,'col'=8] {'col'}, dimensions={0}, use_global_device_ids=true | all-gather | bytes 589824 | tf_op jit(solution)/shard_map/all_gather | solution.py:22
  131.6 2.6 fusion.46
  134.2 2.2 convolution_bitcast_fusion
  136.4 2.9 copy.15
  139.3 24.8 %scatter_custom_fusion = f32[8192,128]{1,0:T(8,128)} fusion(s32[4096]{0:T(1024)S(1)} %bitcast.55, f32[4096,128]{1,0:T(8,128)} %copy.15, f32[]{:T(128)} %constant.126.clone.1), kind=kCustom, calls=%fused_computation.34 | custom fusion | flops 524288 | bytes 4194816 | tf_op jit(solution)/shard_map/scatter-add | solution.py:67
  164.2 87.4 %reduce-scatter.5.cloned.1.call-done = f32[1024,128]{1,0:T(8,128)} async-done(((f32[8192,128]{1,0:T(8,128)}), f32[1024,128]{1,0:T(8,128)}) %reduce-scatter.5.cloned.1.call-update) | async-done | bytes 524304 | tf_op jit(solution)/shard_map/reduce_scatter | solution.py:18
  255.2 2.4 collective-permute-done.1
  259.0 31.6 %all_gather.20 = bf16[2048,128]{1,0:T(8,128)(2,1)S(1)} all-gather(bf16[256,128]{1,0:T(8,128)(2,1)S(1)} %fusion.64), channel_id=1, replica_groups=mesh['row'=4,'col'=8] {'col'}, dimensions={0}, use_global_device_ids=true | all-gather | bytes 589824 | tf_op jit(solution)/shard_map/all_gather | solution.py:22
  294.3 23.8 %collective-permute-done.4 = bf16[4096,128]{1,0:T(8,128)(2,1)} collective-permute-done((bf16[4096,128]{1,0:T(8,128)(2,1)S(1)}, bf16[4096,128]{1,0:T(8,128)(2,1)}, u32[]{:S(2)}, u32[]{:S(2)}) %collective-permute-start.4) | collective-permute-done | bytes 1048608 | tf_op jit(solution)/shard_map/ppermute | solution.py:14
  318.2 4.5 fusion.43
  322.7 31.7 %all_gather.21 = bf16[2048,128]{1,0:T(8,128)(2,1)S(1)} all-gather(bf16[256,128]{1,0:T(8,128)(2,1)S(1)} %fusion.43), channel_id=1, replica_groups=mesh['row'=4,'col'=8] {'col'}, dimensions={0}, use_global_device_ids=true | all-gather | bytes 589824 | tf_op jit(solution)/shard_map/all_gather | solution.py:22
  358.1 23.7 %collective-permute-done.6 = bf16[4096,128]{1,0:T(8,128)(2,1)S(1)} collective-permute-done((bf16[4096,128]{1,0:T(8,128)(2,1)S(1)}, bf16[4096,128]{1,0:T(8,128)(2,1)S(1)}, u32[]{:S(2)}, u32[]{:S(2)}) %collective-permute-start.6) | collective-permute-done | bytes 1048608 | tf_op jit(solution)/shard_map/ppermute | solution.py:14
  383.6 31.3 %all_gather.22 = bf16[2048,128]{1,0:T(8,128)(2,1)S(1)} all-gather(bf16[256,128]{1,0:T(8,128)(2,1)S(1)} %get-tuple-element.4), channel_id=1, replica_groups=mesh['row'=4,'col'=8] {'col'}, dimensions={0}, use_global_device_ids=true | all-gather | bytes 589824 | tf_op jit(solution)/shard_map/all_gather | solution.py:22
  415.0 1.9 collective-permute-done.7
  418.8 23.7 %collective-permute-done.8 = bf16[4096,128]{1,0:T(8,128)(2,1)S(1)} collective-permute-done((bf16[4096,128]{1,0:T(8,128)(2,1)S(1)}, bf16[4096,128]{1,0:T(8,128)(2,1)S(1)}, u32[]{:S(2)}, u32[]{:S(2)}) %collective-permute-start.8) | collective-permute-done | bytes 1048608 | tf_op jit(solution)/shard_map/ppermute | solution.py:14
  444.3 12.9 %gather_fusion.2 = bf16[4096,128]{1,0:T(8,128)(2,1)S(1)} fusion(bf16[8192,128]{1,0:T(8,128)(2,1)} %maximum_select_fusion.4, s32[4096]{0:T(1024)S(1)} %broadcast_clamp_fusion), kind=kCustom, calls=%fused_computation.2 | custom fusion | bytes 2113536 | tf_op jit(solution)/shard_map/gather | solution.py:156
  457.2 2.3 fusion.49
  459.5 31.4 %all_gather.23 = bf16[2048,128]{1,0:T(8,128)(2,1)S(1)} all-gather(bf16[256,128]{1,0:T(8,128)(2,1)S(1)} %fusion.49), channel_id=1, replica_groups=mesh['row'=4,'col'=8] {'col'}, dimensions={0}, use_global_device_ids=true | all-gather | bytes 589824 | tf_op jit(solution)/shard_map/all_gather | solution.py:22
  490.9 1.9 collective-permute-done.9
  492.8 2.6 fusion.14
  (60 shorter events, 25.4 us)
Async XLA Ops:
  7.2 127.0 %copy-start = (bf16[4096,256]{1,0:T(8,128)(2,1)S(1)}, bf16[4096,256]{1,0:T(8,128)(2,1)}, u32[]{:S(2)}) copy-start(bf16[4096,256]{1,0:T(8,128)(2,1)} %param.15) | copy-start | bytes 6291460
  7.2 89.1 %reduce-scatter.3.cloned.1.call-start = ((), (), s32[]{:S(2)}) async-start(), calls=%async_computation.2 | async-start | bytes 2359296 | tf_op jit(solution)/shard_map/reduce_scatter | solution.py:18
  27.0 0.7 copy-start.5
  27.0 69.3 %copy-start.3 = (f32[512,128]{1,0:T(8,128)S(1)}, f32[512,128]{1,0:T(8,128)}, u32[]{:S(2)}) copy-start(f32[512,128]{1,0:T(8,128)} %param.10) | copy-start | bytes 786436
  27.0 102.7 %copy-start.4 = (s32[1,8192]{1,0:T(1,128)S(1)}, s32[1,8192]{1,0:T(1,128)}, u32[]{:S(2)}) copy-start(s32[1,8192]{1,0:T(1,128)} %param.17) | copy-start | bytes 98308
  27.0 224.5 %reduce-scatter.5.cloned.1.call-start = ((), (), s32[]{:S(2)}) async-start(), calls=%async_computation.3 | async-start | bytes 4718592 | tf_op jit(solution)/shard_map/reduce_scatter | solution.py:18
  97.3 36.9 %copy-start.1 = (f32[512,128]{1,0:T(8,128)}, f32[512,128]{1,0:T(8,128)S(1)}, u32[]{:S(2)}) copy-start(f32[512,128]{1,0:T(8,128)S(1)} %sub.36) | copy-start | bytes 786436
  129.7 1.9 collective-permute-start
  252.6 5.0 %collective-permute-start.1 = (bf16[2,256,128]{2,1,0:T(8,128)(2,1)S(1)}, bf16[2,256,128]{2,1,0:T(8,128)(2,1)S(1)}, u32[]{:S(2)}, u32[]{:S(2)}) collective-permute-start(bf16[2,256,128]{2,1,0:T(8,128)(2,1)S(1)} %bitcast.53), channel_id=1, source_target_pairs={{0,16},{16,0},{8,24},{24,8},{1,17},{17,1},{9,25},{25,9},{2,18},{18... | collective-permute-start | bytes 393224 | tf_op jit(solution)/shard_map/ppermute | solution.py:14
  257.7 1.3 collective-permute-start.2
  290.6 1.9 collective-permute-start.3
  292.8 25.4 %collective-permute-start.4 = (bf16[4096,128]{1,0:T(8,128)(2,1)S(1)}, bf16[4096,128]{1,0:T(8,128)(2,1)}, u32[]{:S(2)}, u32[]{:S(2)}) collective-permute-start(bf16[4096,128]{1,0:T(8,128)(2,1)S(1)} %maximum_select_fusion.11), channel_id=1, source_target_pairs={{0,16},{16,0},{8,24},{24,8},{1,17},{17,1},{9,25},{25,9},{2,18},{18... | collective-permute-start | bytes 3145736 | tf_op jit(solution)/shard_map/ppermute | solution.py:14
  294.3 87.5 %slice-start = ((s8[6291456]{0:T(1024)(128)(4,1)}), s8[4194304]{0:T(1024)(128)(4,1)S(1)}, s32[]{:S(2)}) async-start(s8[6291456]{0:T(1024)(128)(4,1)} %bitcast.56), calls=%async_computation.4 | async-start | bytes 8388608
  294.3 87.5 %slice-start.1 = ((s8[6291456]{0:T(1024)(128)(4,1)}), s8[2097152]{0:T(1024)(128)(4,1)S(1)}, s32[]{:S(2)}) async-start(s8[6291456]{0:T(1024)(128)(4,1)} %bitcast.56), calls=%async_computation.5 | async-start | bytes 4194304
  354.4 1.9 collective-permute-start.5
  356.6 25.3 %collective-permute-start.6 = (bf16[4096,128]{1,0:T(8,128)(2,1)S(1)}, bf16[4096,128]{1,0:T(8,128)(2,1)S(1)}, u32[]{:S(2)}, u32[]{:S(2)}) collective-permute-start(bf16[4096,128]{1,0:T(8,128)(2,1)S(1)} %maximum_select_fusion.12), channel_id=1, source_target_pairs={{0,16},{16,0},{8,24},{24,8},{1,17},{17,1},{9,25},{25,9},{2,18},{18... | collective-permute-start | bytes 3145736 | tf_op jit(solution)/shard_map/ppermute | solution.py:14
  415.0 1.9 collective-permute-start.7
  417.2 25.3 %collective-permute-start.8 = (bf16[4096,128]{1,0:T(8,128)(2,1)S(1)}, bf16[4096,128]{1,0:T(8,128)(2,1)S(1)}, u32[]{:S(2)}, u32[]{:S(2)}) collective-permute-start(bf16[4096,128]{1,0:T(8,128)(2,1)S(1)} %maximum_select_fusion.13), channel_id=1, source_target_pairs={{0,16},{16,0},{8,24},{24,8},{1,17},{17,1},{9,25},{25,9},{2,18},{18... | collective-permute-start | bytes 3145736 | tf_op jit(solution)/shard_map/ppermute | solution.py:14
  490.9 4.6 copy-start.2
  490.9 1.9 collective-permute-start.9
Sparse Core Ops, SparseCore 0:
  27.1 69.1 reduce-scatter.2
  164.3 87.2 reduce-scatter.4
where the time goes:
time: 504 us; the launch traced here: 503 us
  waiting for transfers between devices  240 us (48%)
  blocking collectives  166 us (33%)
  other arithmetic  33.5 us (7%)
  matrix products  22.1 us (4%)
  local copies, waits for them, and re-layouts  20.7 us (4%)
  between operations  14.3 us (3%)
  starting transfers between devices  6.39 us (1%)
    all_gather x5, blocking collectives, column_gather(): return lax.all_gather(values, 'col', axis=0, tiled=True)  157 us
    reduce_scatter x2, waiting for transfers between devices, column_sum(): return lax.psum_scatter(values, 'col', scatter_dimension=0, tiled=True)  156 us
    ppermute x10, waiting for transfers between devices, from_partner(): return lax.ppermute(block, axis, route)  84.1 us
    scatter-add x1, other arithmetic, front_reduce(): summed = column_sum(zeros_sum.at[placed].add(partials))  24.8 us
    gather x1, local copies, waits for them, and re-layouts, on_device(): picked_rows = parent_full[targets_all[depth_k]]  12.9 us
    dot_general x4, matrix products, triangle_rows(): return jnp.dot(masked, full_vector, preferred_element_type=jnp.float32)  11.5 us
  transfers between devices with their start and end apart: 12, of which 12 were waited for; matrix products, arithmetic and copies ran while one was open for 0% of the time, Pallas kernels for 0%

commit v1 on v0

v1 whole, which is shorter than its diff:
```python
import itertools

import jax
import jax.numpy as jnp
from jax import lax
from jax.sharding import PartitionSpec as P

BOTH = ("row", "col")


def flip_bit(values, bit):
    count = lax.axis_size("row") * lax.axis_size("col")
    return lax.ppermute(values, BOTH, [(i, i ^ (1 << bit)) for i in range(count)])


def groups_of(bits):
    count = lax.axis_size("row") * lax.axis_size("col")
    mask = sum(1 << b for b in bits)
    groups = []
    for base in range(count):
        if base & mask:
            continue
        group = []
        for choice in itertools.product((0, 1), repeat=len(bits)):
            group.append(base | sum(c << b for c, b in zip(choice, bits)))
        groups.append(group)
    return groups


def exchange(values, bits):
    return lax.all_to_all(values, BOTH, 0, 0, axis_index_groups=groups_of(bits))


def ordered(own, other, bit_value):
    raised = bit_value == 1
    return jnp.stack([jnp.where(raised, other, own), jnp.where(raised, own, other)])


def half(values, wanted):
    return jnp.where(wanted == 1, values[1], values[0])


def front_gather(values, bit_count):
    col_bits = lax.axis_size("col").bit_length() - 1
    row = lax.axis_index("row")
    col = lax.axis_index("col")
    seg_rows, width = values.shape
    upper = [col_bits + b for b in reversed(range(1, bit_count))]
    near = list(reversed(range(col_bits)))
    if upper:
        far = near[0]
        near = near[1:]
        values = ordered(values, flip_bit(values, far), col >> far & 1)
        far_count = 2
    else:
        values = values[None]
        far_count = 1
    count = 2 ** (len(upper) + len(near))
    spread = jnp.broadcast_to(values[None], (count,) + values.shape)
    arrived = exchange(spread, upper + near)
    both = ordered(arrived, flip_bit(arrived, col_bits), row & 1)
    both = both.reshape(2, 2 ** len(upper), 2 ** len(near), far_count, seg_rows, width)
    return both.transpose(1, 0, 3, 2, 4, 5).reshape(-1, width)


def front_reduce(placed, bit_count):
    col_bits = lax.axis_size("col").bit_length() - 1
    row = lax.axis_index("row")
    col = lax.axis_index("col")
    width = placed.shape[1]
    upper = [col_bits + b for b in reversed(range(1, bit_count))]
    far = col_bits - 1
    near = list(reversed(range(far)))
    parts = placed.reshape(2 ** len(upper), 2, 2, 2 ** len(near), -1, width)
    parts = parts.transpose(1, 0, 3, 2, 4, 5)
    core = row & 1
    other = flip_bit(half(parts, 1 - core).astype(jnp.bfloat16), col_bits)
    kept = half(parts, core) + other.astype(jnp.float32)
    kept = kept.reshape((-1,) + kept.shape[2:])
    arrived = exchange(kept.astype(jnp.bfloat16), upper + near)
    return far_sum(arrived, far)


def far_sum(arrived, far):
    side = lax.axis_index("col") >> far & 1
    summed = jnp.sum(arrived.astype(jnp.float32), axis=0)
    other = flip_bit(half(summed, 1 - side).astype(jnp.bfloat16), far)
    return half(summed, side) + other.astype(jnp.float32)


def column_reduce(values):
    col_bits = lax.axis_size("col").bit_length() - 1
    far = col_bits - 1
    near = list(reversed(range(far)))
    width = values.shape[1]
    parts = values.astype(jnp.bfloat16).reshape(2, 2 ** len(near), -1, width).transpose(1, 0, 2, 3)
    return far_sum(exchange(parts, near), far)


def row_gather(values):
    col_bits = lax.axis_size("col").bit_length() - 1
    row_bits = lax.axis_size("row").bit_length() - 1
    pieces = values[None]
    for b in reversed(range(row_bits)):
        pieces = jnp.stack([pieces, flip_bit(pieces, col_bits + b)], 1)
        pieces = pieces.reshape((-1,) + values.shape)
    return pieces


def triangle_rows(tri_panel, full_vector, first_row, strict_lower):
    row_ids = first_row + lax.broadcasted_iota(jnp.int32, tri_panel.shape, 0)
    col_ids = lax.broadcasted_iota(jnp.int32, tri_panel.shape, 1)
    keep_mask = col_ids < row_ids if strict_lower else col_ids >= row_ids
    masked = jnp.where(keep_mask, tri_panel, jnp.zeros_like(tri_panel))
    return jnp.dot(masked, full_vector, preferred_element_type=jnp.float32)


def on_device(
    solution,
    right_side,
    block_values,
    block_columns,
    row_order,
    tri_inverses,
    lower_updates,
    upper_updates,
    update_rows,
):
    row_count = lax.axis_size("row")
    col_count = lax.axis_size("col")
    levels_count = row_count.bit_length() - 1
    per_device = solution.shape[0]
    seg_rows = per_device // levels_count
    block_size = block_values.shape[2]
    per_block = per_device // block_size
    row_index = lax.axis_index("row")
    col_index = lax.axis_index("col")
    gathered = row_gather(solution.astype(jnp.bfloat16))
    owner = block_columns // (per_block * col_count) ^ row_index
    local_block = owner * per_block + block_columns % per_block
    solution_blocks = gathered.reshape(row_count * per_block, block_size, -1)
    picked = solution_blocks[local_block]
    applied = jnp.einsum(
        "iskl,isln->ikn", block_values, picked, preferred_element_type=jnp.float32
    )
    product = column_reduce(applied.reshape(-1, applied.shape[-1]))
    residual = right_side - product
    device_index = row_index * col_count + col_index
    local_order = row_order - device_index * per_device
    permuted = residual[local_order]
    stacked = permuted.reshape(levels_count, seg_rows, -1)
    sep_bottom = 2 * col_count * seg_rows
    lowered = []
    targets_all = []
    first_rows = []
    incoming = None
    for depth_k in range(levels_count):
        groups = 2 ** (depth_k + 1)
        span_rows = sep_bottom * 2**depth_k
        offset_col = sep_bottom * (2**depth_k - 1)
        first_row = (row_index % groups * col_count + col_index) * seg_rows
        first_rows.append(first_row)
        current = stacked[depth_k]
        if depth_k > 0:
            current = current - incoming
        rounded = current.astype(jnp.bfloat16)
        front_full = front_gather(rounded, depth_k + 1)
        tri_panel = tri_inverses[:, offset_col : offset_col + span_rows]
        solved_rows = triangle_rows(tri_panel, front_full, first_row, True) + rounded.astype(
            jnp.float32
        )
        lower_rows = solved_rows.astype(jnp.bfloat16)
        lowered.append(lower_rows)
        if depth_k + 1 < levels_count:
            front_idx = row_index // groups
            chosen = lax.dynamic_slice_in_dim(
                update_rows[depth_k], front_idx * span_rows, span_rows
            )
            targets_all.append(chosen)
            partials = jnp.dot(
                lower_updates[offset_col : offset_col + span_rows],
                lower_rows,
                preferred_element_type=jnp.float32,
            )
            placed = jnp.zeros((2 * span_rows, partials.shape[1]), jnp.float32)
            placed = placed.at[chosen].add(partials)
            incoming = front_reduce(placed, depth_k + 2)
    corrections = [None] * levels_count
    parent_rows = None
    for depth_k in reversed(range(levels_count)):
        span_rows = sep_bottom * 2**depth_k
        offset_col = sep_bottom * (2**depth_k - 1)
        rounded = lowered[depth_k]
        if depth_k + 1 < levels_count:
            parent_full = front_gather(parent_rows, depth_k + 2)
            picked_rows = parent_full[targets_all[depth_k]]
            reduced = rounded.astype(jnp.float32) - jnp.dot(
                upper_updates[:, offset_col : offset_col + span_rows],
                picked_rows,
                preferred_element_type=jnp.float32,
            )
            rounded = reduced.astype(jnp.bfloat16)
        full_vector = front_gather(rounded, depth_k + 1)
        tri_panel = tri_inverses[:, offset_col : offset_col + span_rows]
        upper_rows = triangle_rows(tri_panel, full_vector, first_rows[depth_k], False)
        corrections[depth_k] = upper_rows
        parent_rows = upper_rows.astype(jnp.bfloat16)
    correction = jnp.concatenate(corrections, 0)
    return (solution + correction, residual)


def solution(mesh):
    in_specs = (
        P(BOTH, None),
        P(BOTH, None),
        P("row", "col", None, None),
        P("row", "col"),
        P(BOTH),
        P(BOTH, None),
        P(None, BOTH),
        P(BOTH, None),
        P(),
    )
    out_specs = (P(BOTH, None), P(BOTH, None))
    return jax.shard_map(
        on_device, mesh=mesh, in_specs=in_specs, out_specs=out_specs, check_vma=False
    )
```

time: 504 us -> 255 us (0.51)
  waiting for transfers between devices: 240 us -> 72.1 us
  blocking collectives: 166 us -> 87.8 us
  between operations: 14.3 us -> 1.04 us
  starting transfers between devices: 6.39 us -> 19.1 us
  local copies, waits for them, and re-layouts: 20.7 us -> 27.1 us
  matrix products: 22.1 us -> 16.7 us
    all_gather x6 -> x0, blocking collectives: 166 us -> none  [the longest x5 157 us: column_gather(): return lax.all_gather(values, 'col', axis=0, tiled=True)]
    reduce_scatter x2 -> x0, waiting for transfers between devices: 156 us -> none  [column_sum(): return lax.psum_scatter(values, 'col', scatter_dimension=0, tiled=True)]
    all_to_all x0 -> x5, blocking collectives: none -> 87.8 us  [exchange(): return lax.all_to_all(values, BOTH, 0, 0, axis_index_groups=groups_of(bits))]
    ppermute x10 -> x13, waiting for transfers between devices: 84.1 us -> 43.7 us  [flip_bit(): return lax.ppermute(values, BOTH, [(i, i ^ 1 << bit) for i in range(count)])]
    all_to_all x0 -> x2, waiting for transfers between devices: none -> 28.4 us  [exchange(): return lax.all_to_all(values, BOTH, 0, 0, axis_index_groups=groups_of(bits))]
    all_to_all x0 -> x2, starting transfers between devices: none -> 9.17 us  [exchange(): return lax.all_to_all(values, BOTH, 0, 0, axis_index_groups=groups_of(bits))]
  transfers between devices with their start and end apart: 12 -> 15, of which waited for: 12 -> 15; matrix products, arithmetic and copies ran while one was open for 0% -> 0% of each run, Pallas kernels for 0% -> 0%
where the time goes in v1:
time: 255 us; the launch traced here: 254 us
  blocking collectives  87.8 us (34%)
  waiting for transfers between devices  72.1 us (28%)
  other arithmetic  30.7 us (12%)
  local copies, waits for them, and re-layouts  27.1 us (11%)
  starting transfers between devices  19.1 us (7%)
  matrix products  16.7 us (7%)
    all_to_all x5, blocking collectives, exchange(): return lax.all_to_all(values, BOTH, 0, 0, axis_index_groups=groups_of(bits))  87.8 us
    ppermute x13, waiting for transfers between devices, flip_bit(): return lax.ppermute(values, BOTH, [(i, i ^ 1 << bit) for i in range(count)])  43.7 us
    all_to_all x2, waiting for transfers between devices, exchange(): return lax.all_to_all(values, BOTH, 0, 0, axis_index_groups=groups_of(bits))  28.4 us
    scatter-add x1, other arithmetic, on_device(): placed = placed.at[chosen].add(partials)  24.5 us
    gather x1, local copies, waits for them, and re-layouts, on_device(): picked_rows = parent_full[targets_all[depth_k]]  12.1 us
    ppermute x13, starting transfers between devices, flip_bit(): return lax.ppermute(values, BOTH, [(i, i ^ 1 << bit) for i in range(count)])  9.9 us
    all_to_all x2, starting transfers between devices, exchange(): return lax.all_to_all(values, BOTH, 0, 0, axis_index_groups=groups_of(bits))  9.17 us
    dot_general x4, matrix products, triangle_rows(): return jnp.dot(masked, full_vector, preferred_element_type=jnp.float32)  7.54 us
  transfers between devices with their start and end apart: 15, of which 15 were waited for; matrix products, arithmetic and copies ran while one was open for 0% of the time, Pallas kernels for 0%

profile of v1, /device:TPU:0, one launch (start us, length us, event | category | flops | bytes accessed | tf_op | source)
XLA Modules:
  0.0 254.5 jit_solution(7457229101742785346)
XLA Ops:
  1.8 3.0 %collective-permute-start = (bf16[1,512,128]{2,1,0:T(8,128)(2,1)S(1)}, bf16[1,512,128]{2,1,0:T(8,128)(2,1)S(1)}, u32[]{:S(2)}, u32[]{:S(2)}) collective-permute-start(bf16[1,512,128]{2,1,0:T(8,128)(2,1)S(1)} %get-tuple-element.13), channel_id=1, source_target_pairs={{0,16},{1,17},{2,18},{3,19},{4,20},{5,21},{6,22},{7,23},{8,24},{9,... | collective-permute-start | bytes 393224 | tf_op jit(solution)/shard_map/ppermute | solution.py:13
  4.8 3.5 %collective-permute-done = bf16[1,512,128]{2,1,0:T(8,128)(2,1)S(1)} collective-permute-done((bf16[1,512,128]{2,1,0:T(8,128)(2,1)S(1)}, bf16[1,512,128]{2,1,0:T(8,128)(2,1)S(1)}, u32[]{:S(2)}, u32[]{:S(2)}) %collective-permute-start) | collective-permute-done | bytes 131104 | tf_op jit(solution)/shard_map/ppermute | solution.py:13
  10.0 3.0 %gather_fusion = bf16[128,128,128]{2,1,0:T(8,128)(2,1)} fusion(bf16[16,128,128]{2,1,0:T(8,128)(2,1)S(1)} %bitcast.119, s32[1024]{0:T(1024)S(1)} %pad_clamp_fusion.1), kind=kCustom, calls=%fused_computation | custom fusion | bytes 8389120 | tf_op jit(solution)/shard_map/gather | solution.py:142
  13.0 4.7 %bitcast_convert_fusion = bf16[32,128,128]{1,2,0:T(8,128)(2,1)S(1)} fusion(bf16[32,4,128,128]{3,2,1,0:T(8,128)(2,1)} %param.11, bf16[32,4,128,128]{3,2,1,0:T(8,128)(2,1)} %bitcast.122), kind=kOutput, calls=%fused_computation.27 | convolution fusion | flops 537395200 | bytes 9437184 | tf_op jit(solution)/shard_map/iskl,isln->ikn/dot_general | solution.py:143
  18.8 4.2 %all-to-all-start = ((bf16[4,2,512,128]{3,2,1,0:T(8,128)(2,1)}), bf16[4,2,512,128]{3,2,1,0:T(8,128)(2,1)S(1)}, u32[]{:S(2)}, u32[]{:S(2)}) async-start(bf16[4,2,512,128]{3,2,1,0:T(8,128)(2,1)} %bitcast.127), calls=%async_computation | async-start | bytes 2097152 | tf_op jit(solution)/shard_map/all_to_all | solution.py:31
  23.0 13.9 %all-to-all-done = bf16[4,2,512,128]{3,2,1,0:T(8,128)(2,1)S(1)} async-done(((bf16[4,2,512,128]{3,2,1,0:T(8,128)(2,1)}), bf16[4,2,512,128]{3,2,1,0:T(8,128)(2,1)S(1)}, u32[]{:S(2)}, u32[]{:S(2)}) %all-to-all-start) | async-done | bytes 1048608 | tf_op jit(solution)/shard_map/all_to_all | solution.py:31
  37.9 2.7 %collective-permute-start.2 = (bf16[512,128]{1,0:T(8,128)(2,1)S(1)}, bf16[512,128]{1,0:T(8,128)(2,1)S(1)}, u32[]{:S(2)}, u32[]{:S(2)}) collective-permute-start(bf16[512,128]{1,0:T(8,128)(2,1)S(1)} %fusion.40), channel_id=1, source_target_pairs={{0,4},{1,5},{2,6},{3,7},{4,0},{5,1},{6,2},{7,3},{8,12},{9,13},{10,... | collective-permute-start | bytes 393224 | tf_op jit(solution)/shard_map/ppermute | solution.py:13
  40.6 6.0 %collective-permute-done.2 = bf16[512,128]{1,0:T(8,128)(2,1)S(1)} collective-permute-done((bf16[512,128]{1,0:T(8,128)(2,1)S(1)}, bf16[512,128]{1,0:T(8,128)(2,1)S(1)}, u32[]{:S(2)}, u32[]{:S(2)}) %collective-permute-start.2) | collective-permute-done | bytes 131104 | tf_op jit(solution)/shard_map/ppermute | solution.py:13
  49.6 5.0 %all-to-all-start.1 = ((bf16[8,1,256,128]{3,2,1,0:T(8,128)(2,1)}), bf16[8,1,256,128]{3,2,1,0:T(8,128)(2,1)S(1)}, u32[]{:S(2)}, u32[]{:S(2)}) async-start(bf16[8,1,256,128]{3,2,1,0:T(8,128)(2,1)} %broadcast_in_dim.21), calls=%async_computation.1 | async-start | bytes 1048576 | tf_op jit(solution)/shard_map/all_to_all | solution.py:31
  54.6 14.4 %all-to-all-done.1 = bf16[8,1,256,128]{3,2,1,0:T(8,128)(2,1)S(1)} async-done(((bf16[8,1,256,128]{3,2,1,0:T(8,128)(2,1)}), bf16[8,1,256,128]{3,2,1,0:T(8,128)(2,1)S(1)}, u32[]{:S(2)}, u32[]{:S(2)}) %all-to-all-start.1) | async-done | bytes 524320 | tf_op jit(solution)/shard_map/all_to_all | solution.py:31
  77.6 24.5 %scatter_custom_fusion = f32[8192,128]{1,0:T(8,128)} fusion(s32[4096]{0:T(1024)S(1)} %bitcast.141, f32[4096,128]{1,0:T(8,128)S(1)} %copy.56, f32[]{:T(128)} %constant.86.clone.1), kind=kCustom, calls=%fused_computation.30 | custom fusion | flops 524288 | bytes 4194308 | tf_op jit(solution)/shard_map/scatter-add | solution.py:186
  107.9 19.2 %all_to_all.35 = bf16[8,2,256,128]{3,2,1,0:T(8,128)(2,1)S(1)} all-to-all(bf16[8,2,256,128]{3,2,1,0:T(8,128)(2,1)S(1)} %bitcast.125), channel_id=1, replica_groups={{0,1,2,3,16,17,18,19},{4,5,6,7,20,21,22,23},{8,9,10,11,24,25,26,27},{12..., dimensions={0} | all-to-all | bytes 2097152 | tf_op jit(solution)/shard_map/all_to_all | solution.py:31
  128.8 4.1 %collective-permute-done.5 = bf16[256,128]{1,0:T(8,128)(2,1)S(1)} collective-permute-done((bf16[256,128]{1,0:T(8,128)(2,1)S(1)}, bf16[256,128]{1,0:T(8,128)(2,1)S(1)}, u32[]{:S(2)}, u32[]{:S(2)}) %collective-permute-start.5) | collective-permute-done | bytes 65568 | tf_op jit(solution)/shard_map/ppermute | solution.py:13
  134.0 4.1 %collective-permute-done.6 = bf16[256,128]{1,0:T(8,128)(2,1)S(1)} collective-permute-done((bf16[256,128]{1,0:T(8,128)(2,1)S(1)}, bf16[256,128]{1,0:T(8,128)(2,1)S(1)}, u32[]{:S(2)}, u32[]{:S(2)}) %collective-permute-start.6) | collective-permute-done | bytes 65568 | tf_op jit(solution)/shard_map/ppermute | solution.py:13
  138.4 14.7 %all_to_all.36 = bf16[8,2,256,128]{3,2,1,0:T(8,128)(2,1)S(1)} all-to-all(bf16[8,2,256,128]{3,2,1,0:T(8,128)(2,1)S(1)} %broadcast_in_dim.23), channel_id=1, replica_groups={{0,1,2,3,16,17,18,19},{4,5,6,7,20,21,22,23},{8,9,10,11,24,25,26,27},{12..., dimensions={0} | all-to-all | bytes 2097152 | tf_op jit(solution)/shard_map/all_to_all | solution.py:31
  153.1 2.7 %collective-permute-done.7 = bf16[8,2,256,128]{3,2,1,0:T(8,128)(2,1)S(1)} collective-permute-done((bf16[8,2,256,128]{3,2,1,0:T(8,128)(2,1)S(1)}, bf16[8,2,256,128]{3,2,1,0:T(8,128)(2,1)S(1)}, u32[]{:S(2)}, u32[]{:S(2)}) %collective-permute-start.7) | collective-permute-done | bytes 1048608 | tf_op jit(solution)/shard_map/ppermute | solution.py:13
  161.2 5.1 %collective-permute-done.8 = bf16[256,128]{1,0:T(8,128)(2,1)S(1)} collective-permute-done((bf16[256,128]{1,0:T(8,128)(2,1)S(1)}, bf16[256,128]{1,0:T(8,128)(2,1)S(1)}, u32[]{:S(2)}, u32[]{:S(2)}) %collective-permute-start.8) | collective-permute-done | bytes 65568 | tf_op jit(solution)/shard_map/ppermute | solution.py:13
  166.6 18.2 %all_to_all.37 = bf16[8,2,256,128]{3,2,1,0:T(8,128)(2,1)S(1)} all-to-all(bf16[8,2,256,128]{3,2,1,0:T(8,128)(2,1)S(1)} %broadcast_in_dim.48), channel_id=1, replica_groups={{0,1,2,3,16,17,18,19},{4,5,6,7,20,21,22,23},{8,9,10,11,24,25,26,27},{12..., dimensions={0} | all-to-all | bytes 2097152 | tf_op jit(solution)/shard_map/all_to_all | solution.py:31
  184.8 2.7 %collective-permute-done.9 = bf16[8,2,256,128]{3,2,1,0:T(8,128)(2,1)S(1)} collective-permute-done((bf16[8,2,256,128]{3,2,1,0:T(8,128)(2,1)S(1)}, bf16[8,2,256,128]{3,2,1,0:T(8,128)(2,1)S(1)}, u32[]{:S(2)}, u32[]{:S(2)}) %collective-permute-start.9) | collective-permute-done | bytes 1048608 | tf_op jit(solution)/shard_map/ppermute | solution.py:13
  189.4 6.1 %collective-permute-done.10 = bf16[256,128]{1,0:T(8,128)(2,1)S(1)} collective-permute-done((bf16[256,128]{1,0:T(8,128)(2,1)S(1)}, bf16[256,128]{1,0:T(8,128)(2,1)S(1)}, u32[]{:S(2)}, u32[]{:S(2)}) %collective-permute-start.10) | collective-permute-done | bytes 65568 | tf_op jit(solution)/shard_map/ppermute | solution.py:13
  195.7 18.2 %all_to_all.38 = bf16[8,2,256,128]{3,2,1,0:T(8,128)(2,1)S(1)} all-to-all(bf16[8,2,256,128]{3,2,1,0:T(8,128)(2,1)S(1)} %broadcast_in_dim.49), channel_id=1, replica_groups={{0,1,2,3,16,17,18,19},{4,5,6,7,20,21,22,23},{8,9,10,11,24,25,26,27},{12..., dimensions={0} | all-to-all | bytes 2097152 | tf_op jit(solution)/shard_map/all_to_all | solution.py:31
  214.0 2.6 %collective-permute-done.11 = bf16[8,2,256,128]{3,2,1,0:T(8,128)(2,1)S(1)} collective-permute-done((bf16[8,2,256,128]{3,2,1,0:T(8,128)(2,1)S(1)}, bf16[8,2,256,128]{3,2,1,0:T(8,128)(2,1)S(1)}, u32[]{:S(2)}, u32[]{:S(2)}) %collective-permute-start.11) | collective-permute-done | bytes 1048608 | tf_op jit(solution)/shard_map/ppermute | solution.py:13
  217.1 12.1 %gather_fusion.2 = bf16[4096,128]{1,0:T(8,128)(2,1)S(1)} fusion(bf16[8192,128]{1,0:T(8,128)(2,1)S(1)} %bitcast.118, s32[4096]{0:T(1024)S(1)} %broadcast_clamp_fusion), kind=kCustom, calls=%fused_computation.2 | custom fusion | bytes 2113536 | tf_op jit(solution)/shard_map/gather | solution.py:196
  231.7 17.5 %all_to_all.39 = bf16[8,1,256,128]{3,2,1,0:T(8,128)(2,1)S(1)} all-to-all(bf16[8,1,256,128]{3,2,1,0:T(8,128)(2,1)S(1)} %broadcast_in_dim.50), channel_id=1, replica_groups={{0,1,2,3,4,5,6,7},{8,9,10,11,12,13,14,15},{16,17,18,19,20,21,22,23},{24..., dimensions={0} | all-to-all | bytes 1048576 | tf_op jit(solution)/shard_map/all_to_all | solution.py:31
  (94 shorter events, 41.2 us)
Async XLA Ops:
  0.6 72.9 %copy-start = (bf16[4096,256]{1,0:T(8,128)(2,1)S(1)}, bf16[4096,256]{1,0:T(8,128)(2,1)}, u32[]{:S(2)}) copy-start(bf16[4096,256]{1,0:T(8,128)(2,1)} %param.15) | copy-start | bytes 6291460
  1.8 6.5 %collective-permute-start = (bf16[1,512,128]{2,1,0:T(8,128)(2,1)S(1)}, bf16[1,512,128]{2,1,0:T(8,128)(2,1)S(1)}, u32[]{:S(2)}, u32[]{:S(2)}) collective-permute-start(bf16[1,512,128]{2,1,0:T(8,128)(2,1)S(1)} %get-tuple-element.13), channel_id=1, source_target_pairs={{0,16},{1,17},{2,18},{3,19},{4,20},{5,21},{6,22},{7,23},{8,24},{9,... | collective-permute-start | bytes 393224 | tf_op jit(solution)/shard_map/ppermute | solution.py:13
  8.4 1.6 collective-permute-start.1
  18.8 21.8 %copy-start.7 = (s32[512]{0:T(512)S(1)}, s32[512]{0:T(512)}, u32[]{:S(2)}) copy-start(s32[512]{0:T(512)} %param.13) | copy-start | bytes 6148
  18.8 27.8 %copy-start.5 = (f32[512,128]{1,0:T(8,128)S(1)}, f32[512,128]{1,0:T(8,128)}, u32[]{:S(2)}) copy-start(f32[512,128]{1,0:T(8,128)} %param.10) | copy-start | bytes 786436
  18.8 18.1 %all-to-all-start = ((bf16[4,2,512,128]{3,2,1,0:T(8,128)(2,1)}), bf16[4,2,512,128]{3,2,1,0:T(8,128)(2,1)S(1)}, u32[]{:S(2)}, u32[]{:S(2)}) async-start(bf16[4,2,512,128]{3,2,1,0:T(8,128)(2,1)} %bitcast.127), calls=%async_computation | async-start | bytes 2097152 | tf_op jit(solution)/shard_map/all_to_all | solution.py:31
  37.9 8.6 %collective-permute-start.2 = (bf16[512,128]{1,0:T(8,128)(2,1)S(1)}, bf16[512,128]{1,0:T(8,128)(2,1)S(1)}, u32[]{:S(2)}, u32[]{:S(2)}) collective-permute-start(bf16[512,128]{1,0:T(8,128)(2,1)S(1)} %fusion.40), channel_id=1, source_target_pairs={{0,4},{1,5},{2,6},{3,7},{4,0},{5,1},{6,2},{7,3},{8,12},{9,13},{10,... | collective-permute-start | bytes 393224 | tf_op jit(solution)/shard_map/ppermute | solution.py:13
  47.7 21.4 %copy-start.2 = (f32[512,128]{1,0:T(8,128)}, f32[512,128]{1,0:T(8,128)S(1)}, u32[]{:S(2)}) copy-start(f32[512,128]{1,0:T(8,128)S(1)} %fusion.37) | copy-start | bytes 786436
  47.7 21.4 %copy-start.6 = (s32[1,8192]{1,0:T(1,128)S(1)}, s32[1,8192]{1,0:T(1,128)}, u32[]{:S(2)}) copy-start(s32[1,8192]{1,0:T(1,128)} %param.17) | copy-start | bytes 98308
  49.6 19.4 %all-to-all-start.1 = ((bf16[8,1,256,128]{3,2,1,0:T(8,128)(2,1)}), bf16[8,1,256,128]{3,2,1,0:T(8,128)(2,1)S(1)}, u32[]{:S(2)}, u32[]{:S(2)}) async-start(bf16[8,1,256,128]{3,2,1,0:T(8,128)(2,1)} %broadcast_in_dim.21), calls=%async_computation.1 | async-start | bytes 1048576 | tf_op jit(solution)/shard_map/all_to_all | solution.py:31
  69.0 1.9 collective-permute-start.3
  104.8 2.7 %collective-permute-start.4 = (bf16[2,4,2,256,128]{4,3,2,1,0:T(8,128)(2,1)S(1)}, bf16[2,4,2,256,128]{4,3,2,1,0:T(8,128)(2,1)S(1)}, u32[]{:S(2)}, u32[]{:S(2)}) collective-permute-start(bf16[2,4,2,256,128]{4,3,2,1,0:T(8,128)(2,1)S(1)} %fusion.33), channel_id=1, source_target_pairs={{0,8},{1,9},{2,10},{3,11},{4,12},{5,13},{6,14},{7,15},{8,0},{9,1},... | collective-permute-start | bytes 3145736 | tf_op jit(solution)/shard_map/ppermute | solution.py:13
  127.2 5.6 %collective-permute-start.5 = (bf16[256,128]{1,0:T(8,128)(2,1)S(1)}, bf16[256,128]{1,0:T(8,128)(2,1)S(1)}, u32[]{:S(2)}, u32[]{:S(2)}) collective-permute-start(bf16[256,128]{1,0:T(8,128)(2,1)S(1)} %fusion.42), channel_id=1, source_target_pairs={{0,4},{1,5},{2,6},{3,7},{4,0},{5,1},{6,2},{7,3},{8,12},{9,13},{10,... | collective-permute-start | bytes 196616 | tf_op jit(solution)/shard_map/ppermute | solution.py:13
  132.9 5.3 %collective-permute-start.6 = (bf16[256,128]{1,0:T(8,128)(2,1)S(1)}, bf16[256,128]{1,0:T(8,128)(2,1)S(1)}, u32[]{:S(2)}, u32[]{:S(2)}) collective-permute-start(bf16[256,128]{1,0:T(8,128)(2,1)S(1)} %fusion.41), channel_id=1, source_target_pairs={{0,4},{1,5},{2,6},{3,7},{4,0},{5,1},{6,2},{7,3},{8,12},{9,13},{10,... | collective-permute-start | bytes 196616 | tf_op jit(solution)/shard_map/ppermute | solution.py:13
  153.1 2.7 %collective-permute-start.7 = (bf16[8,2,256,128]{3,2,1,0:T(8,128)(2,1)S(1)}, bf16[8,2,256,128]{3,2,1,0:T(8,128)(2,1)S(1)}, u32[]{:S(2)}, u32[]{:S(2)}) collective-permute-start(bf16[8,2,256,128]{3,2,1,0:T(8,128)(2,1)S(1)} %all_to_all.36), channel_id=1, source_target_pairs={{0,8},{1,9},{2,10},{3,11},{4,12},{5,13},{6,14},{7,15},{8,0},{9,1},... | collective-permute-start | bytes 3145736 | tf_op jit(solution)/shard_map/ppermute | solution.py:13
  155.8 2.2 slice-start
  155.9 2.8 %slice-start.1 = ((s8[6291456]{0:T(1024)(128)(4,1)}), s8[2097152]{0:T(1024)(128)(4,1)S(1)}, s32[]{:S(2)}) async-start(s8[6291456]{0:T(1024)(128)(4,1)} %bitcast.143), calls=%async_computation.8 | async-start | bytes 4194304
  160.0 6.3 %collective-permute-start.8 = (bf16[256,128]{1,0:T(8,128)(2,1)S(1)}, bf16[256,128]{1,0:T(8,128)(2,1)S(1)}, u32[]{:S(2)}, u32[]{:S(2)}) collective-permute-start(bf16[256,128]{1,0:T(8,128)(2,1)S(1)} %add_convert_fusion), channel_id=1, source_target_pairs={{0,4},{1,5},{2,6},{3,7},{4,0},{5,1},{6,2},{7,3},{8,12},{9,13},{10,... | collective-permute-start | bytes 196616 | tf_op jit(solution)/shard_map/ppermute | solution.py:13
  184.8 2.7 %collective-permute-start.9 = (bf16[8,2,256,128]{3,2,1,0:T(8,128)(2,1)S(1)}, bf16[8,2,256,128]{3,2,1,0:T(8,128)(2,1)S(1)}, u32[]{:S(2)}, u32[]{:S(2)}) collective-permute-start(bf16[8,2,256,128]{3,2,1,0:T(8,128)(2,1)S(1)} %all_to_all.37), channel_id=1, source_target_pairs={{0,8},{1,9},{2,10},{3,11},{4,12},{5,13},{6,14},{7,15},{8,0},{9,1},... | collective-permute-start | bytes 3145736 | tf_op jit(solution)/shard_map/ppermute | solution.py:13
  189.3 6.2 %collective-permute-start.10 = (bf16[256,128]{1,0:T(8,128)(2,1)S(1)}, bf16[256,128]{1,0:T(8,128)(2,1)S(1)}, u32[]{:S(2)}, u32[]{:S(2)}) collective-permute-start(bf16[256,128]{1,0:T(8,128)(2,1)S(1)} %get-tuple-element.20), channel_id=1, source_target_pairs={{0,4},{1,5},{2,6},{3,7},{4,0},{5,1},{6,2},{7,3},{8,12},{9,13},{10,... | collective-permute-start | bytes 196616 | tf_op jit(solution)/shard_map/ppermute | solution.py:13
  214.0 2.7 %collective-permute-start.11 = (bf16[8,2,256,128]{3,2,1,0:T(8,128)(2,1)S(1)}, bf16[8,2,256,128]{3,2,1,0:T(8,128)(2,1)S(1)}, u32[]{:S(2)}, u32[]{:S(2)}) collective-permute-start(bf16[8,2,256,128]{3,2,1,0:T(8,128)(2,1)S(1)} %all_to_all.38), channel_id=1, source_target_pairs={{0,8},{1,9},{2,10},{3,11},{4,12},{5,13},{6,14},{7,15},{8,0},{9,1},... | collective-permute-start | bytes 3145736 | tf_op jit(solution)/shard_map/ppermute | solution.py:13
  249.1 1.9 collective-permute-start.12
  251.2 2.5 copy-start.4
  251.2 3.3 %copy-start.1 = (bf16[4096,256]{1,0:T(8,128)(2,1)S(1)}, bf16[4096,256]{1,0:T(8,128)(2,1)}, u32[]{:S(2)}) copy-start(bf16[4096,256]{1,0:T(8,128)(2,1)} %param.15) | copy-start | bytes 6291460
  (1 other events, 0.8 us)

commit v2 on v1

v2 whole, which is shorter than its diff:
```python
import functools
import itertools

import jax
import jax.numpy as jnp
from jax import lax
from jax.experimental import pallas as pl
from jax.experimental.pallas import tpu as pltpu
from jax.sharding import PartitionSpec as P

BOTH = ("row", "col")


def flip_bit(values, bit):
    count = lax.axis_size("row") * lax.axis_size("col")
    return lax.ppermute(values, BOTH, [(i, i ^ (1 << bit)) for i in range(count)])


def groups_of(bits):
    count = lax.axis_size("row") * lax.axis_size("col")
    mask = sum(1 << b for b in bits)
    groups = []
    for base in range(count):
        if base & mask:
            continue
        group = []
        for choice in itertools.product((0, 1), repeat=len(bits)):
            group.append(base | sum(c << b for c, b in zip(choice, bits)))
        groups.append(group)
    return groups


def exchange(values, bits):
    return lax.all_to_all(values, BOTH, 0, 0, axis_index_groups=groups_of(bits))


def ordered(own, other, bit_value):
    raised = bit_value == 1
    return jnp.stack([jnp.where(raised, other, own), jnp.where(raised, own, other)])


def col_bit_count():
    return lax.axis_size("col").bit_length() - 1


def near_bits():
    return list(reversed(range(col_bit_count() - 1)))


def upper_bits(bit_count):
    return [col_bit_count() + b for b in reversed(range(1, bit_count))]


def far_side():
    return lax.axis_index("col") >> (col_bit_count() - 1)


def gather_halves(values, bit_count):
    col_bits = col_bit_count()
    other = flip_bit(values, col_bits - 1)
    values = jnp.stack([values, other])
    bits = upper_bits(bit_count) + near_bits()
    spread = jnp.broadcast_to(values[None], (2 ** len(bits),) + values.shape)
    arrived = exchange(spread, bits)
    return arrived, flip_bit(arrived, col_bits)


def arrival_rows(rows, bit_count, seg_rows):
    near_count = 2 ** len(near_bits())
    within = rows % seg_rows
    near = rows // seg_rows % near_count
    far = rows // (seg_rows * near_count) % 2 ^ far_side()
    core = rows // (seg_rows * near_count * 2) % 2 ^ lax.axis_index("row") & 1
    upper = rows // (seg_rows * near_count * 4)
    upper_count = 2 ** (bit_count - 1)
    return (((core * upper_count + upper) * near_count + near) * 2 + far) * seg_rows + within


def front_gather(values, bit_count):
    col_bits = col_bit_count()
    row = lax.axis_index("row")
    seg_rows, width = values.shape
    if bit_count > 1:
        arrived, other = gather_halves(values, bit_count)
        side = far_side()
        pieces = ordered(arrived, other, row & 1)
        pieces = ordered(pieces[:, :, 0], pieces[:, :, 1], side)
        pieces = pieces.reshape(2, 2, 2 ** (bit_count - 1), -1, seg_rows, width)
        return pieces.transpose(2, 1, 0, 3, 4, 5).reshape(-1, width)
    bits = list(reversed(range(col_bits)))
    spread = jnp.broadcast_to(values[None], (2**col_bits,) + values.shape)
    arrived = exchange(spread, bits)
    return ordered(arrived, flip_bit(arrived, col_bits), row & 1).reshape(-1, width)


def far_sum(arrived):
    summed = jnp.sum(arrived.astype(jnp.float32), axis=0)
    other = flip_bit(summed[1].astype(jnp.bfloat16), col_bit_count() - 1)
    return summed[0] + other.astype(jnp.float32)


def front_reduce(kept, sent, bit_count, seg_rows):
    other = flip_bit(sent, col_bit_count())
    total = (kept.astype(jnp.float32) + other.astype(jnp.float32)).astype(jnp.bfloat16)
    bits = upper_bits(bit_count) + near_bits()
    total = total.reshape(2 ** len(bits), 2, seg_rows, -1)
    return far_sum(exchange(total, bits))


def row_gather(values):
    col_bits = col_bit_count()
    row_bits = lax.axis_size("row").bit_length() - 1
    pieces = values[None]
    for b in reversed(range(row_bits)):
        pieces = jnp.stack([pieces, flip_bit(pieces, col_bits + b)], 1)
        pieces = pieces.reshape((-1,) + values.shape)
    return pieces


def product_kernel(near_count, picks_ref, side_ref, values_ref, blocks_ref, out_ref):
    step = pl.program_id(0)
    rows, slots, size, _ = values_ref.shape
    for r in range(rows):
        left = [values_ref[r, s] for s in range(slots)]
        right = [blocks_ref[picks_ref[(step * rows + r) * slots + s]] for s in range(slots)]
        total = jnp.dot(
            jnp.concatenate(left, 1),
            jnp.concatenate(right, 0),
            preferred_element_type=jnp.float32,
        )
        out_ref[pl.ds(r * size, size), :] = total.astype(jnp.bfloat16)


def block_product(values, blocks, picks, per_block):
    block_rows, slots, size, _ = values.shape
    width = blocks.shape[2]
    near_count = 2 ** len(near_bits())
    steps = block_rows // per_block

    def place(i, picks_ref, side_ref):
        return (i % near_count * 2 + (i // near_count ^ side_ref[0]), 0)

    return pl.pallas_call(
        functools.partial(product_kernel, near_count),
        out_shape=jax.ShapeDtypeStruct((block_rows * size, width), jnp.bfloat16),
        grid_spec=pltpu.PrefetchScalarGridSpec(
            num_scalar_prefetch=2,
            grid=(steps,),
            in_specs=[
                pl.BlockSpec((per_block, slots, size, size), lambda i, *_: (i, 0, 0, 0)),
                pl.BlockSpec(blocks.shape, lambda i, *_: (0, 0, 0)),
            ],
            out_specs=pl.BlockSpec((per_block * size, width), place),
        ),
    )(picks.reshape(-1), far_side().reshape(1), values, blocks)


UNROLL = 16


def scatter_kernel(places_ref, lower_ref, rows_ref, kept_ref, sent_ref, part, total):
    step = pl.program_id(0)
    chunk = part.shape[0]

    @pl.when(step == 0)
    def _():
        total[...] = jnp.zeros_like(total)

    part[...] = jnp.dot(lower_ref[...], rows_ref[...], preferred_element_type=jnp.float32)

    def move(i, carry):
        for j in range(UNROLL):
            u = i * UNROLL + j
            total[pl.ds(places_ref[step * chunk + u], 1), :] = part[pl.ds(u, 1), :]
        return carry

    lax.fori_loop(0, chunk // UNROLL, move, 0)

    @pl.when(step == pl.num_programs(0) - 1)
    def _():
        count = kept_ref.shape[0]
        kept_ref[...] = total[:count].astype(jnp.bfloat16)
        sent_ref[...] = total[count:].astype(jnp.bfloat16)


def scatter_update(lower, rows, places):
    span, seg_rows = lower.shape
    width = rows.shape[1]
    chunk = min(span, 512)
    return pl.pallas_call(
        scatter_kernel,
        out_shape=[jax.ShapeDtypeStruct((span, width), jnp.bfloat16)] * 2,
        grid_spec=pltpu.PrefetchScalarGridSpec(
            num_scalar_prefetch=1,
            grid=(span // chunk,),
            in_specs=[
                pl.BlockSpec((chunk, seg_rows), lambda i, *_: (i, 0)),
                pl.BlockSpec((seg_rows, width), lambda i, *_: (0, 0)),
            ],
            out_specs=[pl.BlockSpec((span, width), lambda i, *_: (0, 0))] * 2,
            scratch_shapes=[
                pltpu.VMEM((chunk, width), jnp.float32),
                pltpu.VMEM((2 * span, width), jnp.float32),
            ],
        ),
    )(places, lower, rows)


def pick_kernel(places_ref, upper_ref, own_ref, other_ref, base_ref, out_ref, full, part, total):
    step = pl.program_id(0)
    chunk = part.shape[0]

    @pl.when(step == 0)
    def _():
        count = own_ref.shape[0]
        full[:count] = own_ref[...].astype(jnp.float32)
        full[count:] = other_ref[...].astype(jnp.float32)
        total[...] = base_ref[...].astype(jnp.float32)

    def move(i, carry):
        for j in range(UNROLL):
            u = i * UNROLL + j
            part[pl.ds(u, 1), :] = full[pl.ds(places_ref[step * chunk + u], 1), :]
        return carry

    lax.fori_loop(0, chunk // UNROLL, move, 0)
    total[...] -= jnp.dot(
        upper_ref[...], part[...].astype(jnp.bfloat16), preferred_element_type=jnp.float32
    )

    @pl.when(step == pl.num_programs(0) - 1)
    def _():
        out_ref[...] = total[...].astype(jnp.bfloat16)


def pick_update(upper, own, other, places, base):
    seg_rows, span = upper.shape
    width = base.shape[1]
    chunk = min(span, 512)
    own = own.reshape(-1, width)
    other = other.reshape(-1, width)
    return pl.pallas_call(
        pick_kernel,
        out_shape=jax.ShapeDtypeStruct((seg_rows, width), jnp.bfloat16),
        grid_spec=pltpu.PrefetchScalarGridSpec(
            num_scalar_prefetch=1,
            grid=(span // chunk,),
            in_specs=[
                pl.BlockSpec((seg_rows, chunk), lambda i, *_: (0, i)),
                pl.BlockSpec(own.shape, lambda i, *_: (0, 0)),
                pl.BlockSpec(other.shape, lambda i, *_: (0, 0)),
                pl.BlockSpec((seg_rows, width), lambda i, *_: (0, 0)),
            ],
            out_specs=pl.BlockSpec((seg_rows, width), lambda i, *_: (0, 0)),
            scratch_shapes=[
                pltpu.VMEM((2 * span, width), jnp.float32),
                pltpu.VMEM((chunk, width), jnp.float32),
                pltpu.VMEM((seg_rows, width), jnp.float32),
            ],
        ),
    )(places, upper, own, other, base)


def triangle_rows(tri_panel, full_vector, first_row, strict_lower):
    row_ids = first_row + lax.broadcasted_iota(jnp.int32, tri_panel.shape, 0)
    col_ids = lax.broadcasted_iota(jnp.int32, tri_panel.shape, 1)
    keep_mask = col_ids < row_ids if strict_lower else col_ids >= row_ids
    masked = jnp.where(keep_mask, tri_panel, jnp.zeros_like(tri_panel))
    return jnp.dot(masked, full_vector, preferred_element_type=jnp.float32)


def on_device(
    solution,
    right_side,
    block_values,
    block_columns,
    row_order,
    tri_inverses,
    lower_updates,
    upper_updates,
    update_rows,
):
    row_count = lax.axis_size("row")
    col_count = lax.axis_size("col")
    levels_count = row_count.bit_length() - 1
    per_device = solution.shape[0]
    seg_rows = per_device // levels_count
    block_size = block_values.shape[2]
    per_block = per_device // block_size
    row_index = lax.axis_index("row")
    col_index = lax.axis_index("col")
    gathered = row_gather(solution.astype(jnp.bfloat16))
    owner = block_columns // (per_block * col_count) ^ row_index
    local_block = owner * per_block + block_columns % per_block
    solution_blocks = gathered.reshape(row_count * per_block, block_size, -1)
    applied = block_product(block_values, solution_blocks, local_block, per_block)
    applied = applied.reshape(-1, 2, per_device, applied.shape[-1])
    product = far_sum(exchange(applied, near_bits()))
    residual = right_side - product
    device_index = row_index * col_count + col_index
    local_order = row_order - device_index * per_device
    permuted = residual[local_order]
    stacked = permuted.reshape(levels_count, seg_rows, -1)
    sep_bottom = 2 * col_count * seg_rows
    lowered = []
    targets_all = []
    first_rows = []
    incoming = None
    for depth_k in range(levels_count):
        groups = 2 ** (depth_k + 1)
        span_rows = sep_bottom * 2**depth_k
        offset_col = sep_bottom * (2**depth_k - 1)
        first_row = (row_index % groups * col_count + col_index) * seg_rows
        first_rows.append(first_row)
        current = stacked[depth_k]
        if depth_k > 0:
            current = current - incoming
        rounded = current.astype(jnp.bfloat16)
        front_full = front_gather(rounded, depth_k + 1)
        tri_panel = tri_inverses[:, offset_col : offset_col + span_rows]
        solved_rows = triangle_rows(tri_panel, front_full, first_row, True) + rounded.astype(
            jnp.float32
        )
        lower_rows = solved_rows.astype(jnp.bfloat16)
        lowered.append(lower_rows)
        if depth_k + 1 < levels_count:
            front_idx = row_index // groups
            chosen = lax.dynamic_slice_in_dim(
                update_rows[depth_k], front_idx * span_rows, span_rows
            )
            places = arrival_rows(chosen, depth_k + 2, seg_rows)
            targets_all.append(places)
            kept, sent = scatter_update(
                lower_updates[offset_col : offset_col + span_rows], lower_rows, places
            )
            incoming = front_reduce(kept, sent, depth_k + 2, seg_rows)
    corrections = [None] * levels_count
    parent_rows = None
    for depth_k in reversed(range(levels_count)):
        span_rows = sep_bottom * 2**depth_k
        offset_col = sep_bottom * (2**depth_k - 1)
        rounded = lowered[depth_k]
        if depth_k + 1 < levels_count:
            own, other = gather_halves(parent_rows, depth_k + 2)
            rounded = pick_update(
                upper_updates[:, offset_col : offset_col + span_rows],
                own,
                other,
                targets_all[depth_k],
                rounded,
            )
        full_vector = front_gather(rounded, depth_k + 1)
        tri_panel = tri_inverses[:, offset_col : offset_col + span_rows]
        upper_rows = triangle_rows(tri_panel, full_vector, first_rows[depth_k], False)
        corrections[depth_k] = upper_rows
        parent_rows = upper_rows.astype(jnp.bfloat16)
    correction = jnp.concatenate(corrections, 0)
    return (solution + correction, residual)


def solution(mesh):
    in_specs = (
        P(BOTH, None),
        P(BOTH, None),
        P("row", "col", None, None),
        P("row", "col"),
        P(BOTH),
        P(BOTH, None),
        P(None, BOTH),
        P(BOTH, None),
        P(),
    )
    out_specs = (P(BOTH, None), P(BOTH, None))
    return jax.shard_map(
        on_device, mesh=mesh, in_specs=in_specs, out_specs=out_specs, check_vma=False
    )
```

time: 255 us -> 234 us (0.918)
  Pallas kernels: 0 us -> 30.2 us
  other arithmetic: 30.7 us -> 6.47 us
  local copies, waits for them, and re-layouts: 27.1 us -> 8.88 us
  matrix products: 16.7 us -> 8.06 us
    pallas_call x0 -> x3, Pallas kernels: none -> 30.2 us  [the longest x1 11.3 us: scatter_update(): pl.pallas_call(scatter_kernel, out_shape=[jax.ShapeDtypeStruct((span, wid...]
    scatter-add x1 -> x0, other arithmetic: 24.5 us -> none  [on_device(): placed = placed.at[chosen].add(partials)]
    gather x2 -> x0, local copies, waits for them, and re-layouts: 15.2 us -> none  [the longest x1 12.1 us: on_device(): picked_rows = parent_full[targets_all[depth_k]]]
    dot_general x3 -> x0, matrix products: 9.17 us -> none  [the longest x1 4.71 us: on_device(): jnp.einsum('iskl,isln->ikn', block_values, picked, preferred_element_type...]
  transfers between devices with their start and end apart: 15 -> 15, of which waited for: 15 -> 15; matrix products, arithmetic and copies ran while one was open for 0% -> 1% of each run, Pallas kernels for 0% -> 0%
where the time goes in v2:
time: 234 us; the launch traced here: 233 us
  blocking collectives  87.8 us (38%)
  waiting for transfers between devices  71.2 us (30%)
  Pallas kernels  30.2 us (13%)
  starting transfers between devices  19.1 us (8%)
  local copies, waits for them, and re-layouts  8.88 us (4%)
  matrix products  8.06 us (3%)
  other arithmetic  6.47 us (3%)
    all_to_all x5, blocking collectives, exchange(): return lax.all_to_all(values, BOTH, 0, 0, axis_index_groups=groups_of(bits))  87.8 us
    ppermute x13, waiting for transfers between devices, flip_bit(): return lax.ppermute(values, BOTH, [(i, i ^ 1 << bit) for i in range(count)])  42.8 us
    all_to_all x2, waiting for transfers between devices, exchange(): return lax.all_to_all(values, BOTH, 0, 0, axis_index_groups=groups_of(bits))  28.4 us
    pallas_call x1, Pallas kernels, scatter_update(): pl.pallas_call(scatter_kernel, out_shape=[jax.ShapeDtypeStruct((span, wid...  11.3 us
    pallas_call x1, Pallas kernels, pick_update(): pl.pallas_call(pick_kernel, out_shape=jax.ShapeDtypeStruct((seg_rows, wid...  11.1 us
    ppermute x13, starting transfers between devices, flip_bit(): return lax.ppermute(values, BOTH, [(i, i ^ 1 << bit) for i in range(count)])  9.97 us
    all_to_all x2, starting transfers between devices, exchange(): return lax.all_to_all(values, BOTH, 0, 0, axis_index_groups=groups_of(bits))  9.16 us
    dot_general x4, matrix products, triangle_rows(): return jnp.dot(masked, full_vector, preferred_element_type=jnp.float32)  8.06 us
  transfers between devices with their start and end apart: 15, of which 15 were waited for; matrix products, arithmetic and copies ran while one was open for 1% of the time, Pallas kernels for 0%

profile of v2, /device:TPU:0, one launch (start us, length us, event | category | flops | bytes accessed | tf_op | source)
XLA Modules:
  0.0 232.7 jit_solution(7669309966355965413)
XLA Ops:
  1.6 3.0 %collective-permute-start = (bf16[1,512,128]{2,1,0:T(8,128)(2,1)S(1)}, bf16[1,512,128]{2,1,0:T(8,128)(2,1)S(1)}, u32[]{:S(2)}, u32[]{:S(2)}) collective-permute-start(bf16[1,512,128]{2,1,0:T(8,128)(2,1)S(1)} %get-tuple-element.21), channel_id=1, source_target_pairs={{0,16},{1,17},{2,18},{3,19},{4,20},{5,21},{6,22},{7,23},{8,24},{9,... | collective-permute-start | bytes 393224 | tf_op jit(solution)/shard_map/ppermute | solution.py:16
  4.7 3.5 %collective-permute-done = bf16[1,512,128]{2,1,0:T(8,128)(2,1)S(1)} collective-permute-done((bf16[1,512,128]{2,1,0:T(8,128)(2,1)S(1)}, bf16[1,512,128]{2,1,0:T(8,128)(2,1)S(1)}, u32[]{:S(2)}, u32[]{:S(2)}) %collective-permute-start) | collective-permute-done | bytes 131104 | tf_op jit(solution)/shard_map/ppermute | solution.py:16
  10.7 7.8 %shard_map.104 = bf16[4096,128]{1,0:T(8,128)(2,1)} custom-call(s32[128]{0:T(128)} %reshape.142.picks_ref, s32[1]{0:T(128)} %bitcast.2.side_ref, bf16[32,4,128,128]{3,2,1,0:T(8,128)(2,1)} %values_ref.1, bf16[16,128,128]{2,1,0:T(8,128)(2,1)} %bitcast.86), custom_call_target="tpu_custom_call" | custom-call | tf_op jit(solution)/shard_map/pallas_call | solution.py:143
  18.5 4.2 %all-to-all-start = ((bf16[4,2,512,128]{3,2,1,0:T(8,128)(2,1)}), bf16[4,2,512,128]{3,2,1,0:T(8,128)(2,1)S(1)}, u32[]{:S(2)}, u32[]{:S(2)}) async-start(bf16[4,2,512,128]{3,2,1,0:T(8,128)(2,1)} %bitcast.84), calls=%async_computation | async-start | bytes 2097152 | tf_op jit(solution)/shard_map/all_to_all | solution.py:34
  22.6 14.2 %all-to-all-done = bf16[4,2,512,128]{3,2,1,0:T(8,128)(2,1)S(1)} async-done(((bf16[4,2,512,128]{3,2,1,0:T(8,128)(2,1)}), bf16[4,2,512,128]{3,2,1,0:T(8,128)(2,1)S(1)}, u32[]{:S(2)}, u32[]{:S(2)}) %all-to-all-start) | async-done | bytes 1048608 | tf_op jit(solution)/shard_map/all_to_all | solution.py:34
  37.0 2.6 %collective-permute-start.2 = (bf16[512,128]{1,0:T(8,128)(2,1)S(1)}, bf16[512,128]{1,0:T(8,128)(2,1)S(1)}, u32[]{:S(2)}, u32[]{:S(2)}) collective-permute-start(bf16[512,128]{1,0:T(8,128)(2,1)S(1)} %fusion.36), channel_id=1, source_target_pairs={{0,4},{1,5},{2,6},{3,7},{4,0},{5,1},{6,2},{7,3},{8,12},{9,13},{10,... | collective-permute-start | bytes 393224 | tf_op jit(solution)/shard_map/ppermute | solution.py:16
  39.7 6.0 %collective-permute-done.2 = bf16[512,128]{1,0:T(8,128)(2,1)S(1)} collective-permute-done((bf16[512,128]{1,0:T(8,128)(2,1)S(1)}, bf16[512,128]{1,0:T(8,128)(2,1)S(1)}, u32[]{:S(2)}, u32[]{:S(2)}) %collective-permute-start.2) | collective-permute-done | bytes 131104 | tf_op jit(solution)/shard_map/ppermute | solution.py:16
  47.7 5.0 %all-to-all-start.1 = ((bf16[8,256,128]{2,1,0:T(8,128)(2,1)}), bf16[8,256,128]{2,1,0:T(8,128)(2,1)S(1)}, u32[]{:S(2)}, u32[]{:S(2)}) async-start(bf16[8,256,128]{2,1,0:T(8,128)(2,1)} %broadcast_in_dim.16), calls=%async_computation.1 | async-start | bytes 1048576 | tf_op jit(solution)/shard_map/all_to_all | solution.py:34
  52.6 14.2 %all-to-all-done.1 = bf16[8,256,128]{2,1,0:T(8,128)(2,1)S(1)} async-done(((bf16[8,256,128]{2,1,0:T(8,128)(2,1)}), bf16[8,256,128]{2,1,0:T(8,128)(2,1)S(1)}, u32[]{:S(2)}, u32[]{:S(2)}) %all-to-all-start.1) | async-done | bytes 524320 | tf_op jit(solution)/shard_map/all_to_all | solution.py:34
  69.0 3.0 %fusion.25.rows_ref.base_ref = bf16[256,128]{1,0:T(8,128)(2,1)} fusion(bf16[4096,128]{1,0:T(8,128)(2,1)S(1)} %bitcast.90, s32[256]{0:T(256)S(1)} %iota_add_fusion.1, bf16[256,12288]{1,0:T(8,128)(2,1)} %param.14, f32[512,128]{1,0:T(8,128)S(1)} %gather_fusion), kind=kOutput, calls=%fused_computation.35 | convolution fusion | flops 270630912 | bytes 3277824 | tf_op jit(solution)/shard_map/dot_general | solution.py:269
  72.0 11.3 %shard_map.105 = (bf16[4096,128]{1,0:T(8,128)(2,1)}, bf16[4096,128]{1,0:T(8,128)(2,1)}) custom-call(s32[4096]{0:T(1024)} %fusion.51.places_ref, bf16[4096,256]{1,0:T(8,128)(2,1)} %lower_ref.1, bf16[256,128]{1,0:T(8,128)(2,1)} %fusion.25.rows_ref.base_ref), custom_call_target="tpu_custom_call" | custom-call | tf_op jit(solution)/shard_map/pallas_call | solution.py:190
  83.4 2.7 %collective-permute-done.4 = bf16[4096,128]{1,0:T(8,128)(2,1)S(1)} collective-permute-done((bf16[4096,128]{1,0:T(8,128)(2,1)}, bf16[4096,128]{1,0:T(8,128)(2,1)S(1)}, u32[]{:S(2)}, u32[]{:S(2)}) %collective-permute-start.4) | collective-permute-done | bytes 1048608 | tf_op jit(solution)/shard_map/ppermute | solution.py:16
  87.7 19.1 %all_to_all.35 = bf16[8,2,256,128]{3,2,1,0:T(8,128)(2,1)S(1)} all-to-all(bf16[8,2,256,128]{3,2,1,0:T(8,128)(2,1)S(1)} %bitcast.79), channel_id=1, replica_groups={{0,1,2,3,16,17,18,19},{4,5,6,7,20,21,22,23},{8,9,10,11,24,25,26,27},{12..., dimensions={0} | all-to-all | bytes 2097152 | tf_op jit(solution)/shard_map/all_to_all | solution.py:34
  108.5 4.1 %collective-permute-done.5 = bf16[256,128]{1,0:T(8,128)(2,1)S(1)} collective-permute-done((bf16[256,128]{1,0:T(8,128)(2,1)S(1)}, bf16[256,128]{1,0:T(8,128)(2,1)S(1)}, u32[]{:S(2)}, u32[]{:S(2)}) %collective-permute-start.5) | collective-permute-done | bytes 65568 | tf_op jit(solution)/shard_map/ppermute | solution.py:16
  113.8 4.1 %collective-permute-done.6 = bf16[256,128]{1,0:T(8,128)(2,1)S(1)} collective-permute-done((bf16[256,128]{1,0:T(8,128)(2,1)S(1)}, bf16[256,128]{1,0:T(8,128)(2,1)S(1)}, u32[]{:S(2)}, u32[]{:S(2)}) %collective-permute-start.6) | collective-permute-done | bytes 65568 | tf_op jit(solution)/shard_map/ppermute | solution.py:16
  118.1 14.7 %all_to_all.36 = bf16[8,2,256,128]{3,2,1,0:T(8,128)(2,1)S(1)} all-to-all(bf16[8,2,256,128]{3,2,1,0:T(8,128)(2,1)S(1)} %broadcast_in_dim.17), channel_id=1, replica_groups={{0,1,2,3,16,17,18,19},{4,5,6,7,20,21,22,23},{8,9,10,11,24,25,26,27},{12..., dimensions={0} | all-to-all | bytes 2097152 | tf_op jit(solution)/shard_map/all_to_all | solution.py:34
  141.2 5.1 %collective-permute-done.8 = bf16[256,128]{1,0:T(8,128)(2,1)S(1)} collective-permute-done((bf16[256,128]{1,0:T(8,128)(2,1)S(1)}, bf16[256,128]{1,0:T(8,128)(2,1)S(1)}, u32[]{:S(2)}, u32[]{:S(2)}) %collective-permute-start.8) | collective-permute-done | bytes 65568 | tf_op jit(solution)/shard_map/ppermute | solution.py:16
  146.6 18.2 %all_to_all.37 = bf16[8,2,256,128]{3,2,1,0:T(8,128)(2,1)S(1)} all-to-all(bf16[8,2,256,128]{3,2,1,0:T(8,128)(2,1)S(1)} %broadcast_in_dim.18), channel_id=1, replica_groups={{0,1,2,3,16,17,18,19},{4,5,6,7,20,21,22,23},{8,9,10,11,24,25,26,27},{12..., dimensions={0} | all-to-all | bytes 2097152 | tf_op jit(solution)/shard_map/all_to_all | solution.py:34
  165.0 2.6 %collective-permute-done.9 = bf16[8,2,256,128]{3,2,0,1:T(8,128)(2,1)S(1)} collective-permute-done((bf16[8,2,256,128]{3,2,0,1:T(8,128)(2,1)S(1)}, bf16[8,2,256,128]{3,2,0,1:T(8,128)(2,1)S(1)}, u32[]{:S(2)}, u32[]{:S(2)}) %collective-permute-start.9) | collective-permute-done | bytes 1048608 | tf_op jit(solution)/shard_map/ppermute | solution.py:16
  169.9 6.1 %collective-permute-done.10 = bf16[256,128]{1,0:T(8,128)(2,1)S(1)} collective-permute-done((bf16[256,128]{1,0:T(8,128)(2,1)S(1)}, bf16[256,128]{1,0:T(8,128)(2,1)S(1)}, u32[]{:S(2)}, u32[]{:S(2)}) %collective-permute-start.10) | collective-permute-done | bytes 65568 | tf_op jit(solution)/shard_map/ppermute | solution.py:16
  176.1 18.2 %all_to_all.38 = bf16[8,2,256,128]{3,2,1,0:T(8,128)(2,1)S(1)} all-to-all(bf16[8,2,256,128]{3,2,1,0:T(8,128)(2,1)S(1)} %broadcast_in_dim.19), channel_id=1, replica_groups={{0,1,2,3,16,17,18,19},{4,5,6,7,20,21,22,23},{8,9,10,11,24,25,26,27},{12..., dimensions={0} | all-to-all | bytes 2097152 | tf_op jit(solution)/shard_map/all_to_all | solution.py:34
  194.4 2.7 %collective-permute-done.11 = bf16[8,2,256,128]{3,2,1,0:T(8,128)(2,1)S(1)} collective-permute-done((bf16[8,2,256,128]{3,2,1,0:T(8,128)(2,1)S(1)}, bf16[8,2,256,128]{3,2,1,0:T(8,128)(2,1)S(1)}, u32[]{:S(2)}, u32[]{:S(2)}) %collective-permute-start.11) | collective-permute-done | bytes 1048608 | tf_op jit(solution)/shard_map/ppermute | solution.py:16
  198.0 11.1 %shard_map.106 = bf16[256,128]{1,0:T(8,128)(2,1)} custom-call(s32[4096]{0:T(1024)} %fusion.51.places_ref, bf16[256,4096]{1,0:T(8,128)(2,1)} %upper_ref.1, bf16[4096,128]{1,0:T(8,128)(2,1)} %bitcast.85, bf16[4096,128]{1,0:T(8,128)(2,1)} %bitcast.91, bf16[256,128]{1,0:T(8,128)(2,1)} %fusion.25.rows_ref.base_ref), custom_call_target="tpu_custom_call" | custom-call | tf_op jit(solution)/shard_map/pallas_call | solution.py:242
  210.0 17.5 %all_to_all.39 = bf16[8,256,128]{2,1,0:T(8,128)(2,1)S(1)} all-to-all(bf16[8,256,128]{2,1,0:T(8,128)(2,1)S(1)} %broadcast_in_dim.20), channel_id=1, replica_groups={{0,1,2,3,4,5,6,7},{8,9,10,11,12,13,14,15},{16,17,18,19,20,21,22,23},{24..., dimensions={0} | all-to-all | bytes 1048576 | tf_op jit(solution)/shard_map/all_to_all | solution.py:34
  (82 shorter events, 30.6 us)
Async XLA Ops:
  0.6 66.3 %copy-start = (s32[1,8192]{1,0:T(1,128)S(1)}, s32[1,8192]{1,0:T(1,128)}, u32[]{:S(2)}) copy-start(s32[1,8192]{1,0:T(1,128)} %param.17) | copy-start | bytes 98308
  1.6 6.5 %collective-permute-start = (bf16[1,512,128]{2,1,0:T(8,128)(2,1)S(1)}, bf16[1,512,128]{2,1,0:T(8,128)(2,1)S(1)}, u32[]{:S(2)}, u32[]{:S(2)}) collective-permute-start(bf16[1,512,128]{2,1,0:T(8,128)(2,1)S(1)} %get-tuple-element.21), channel_id=1, source_target_pairs={{0,16},{1,17},{2,18},{3,19},{4,20},{5,21},{6,22},{7,23},{8,24},{9,... | collective-permute-start | bytes 393224 | tf_op jit(solution)/shard_map/ppermute | solution.py:16
  8.2 1.6 collective-permute-start.1
  18.5 21.2 %copy-start.6 = (s32[512]{0:T(512)S(1)}, s32[512]{0:T(512)}, u32[]{:S(2)}) copy-start(s32[512]{0:T(512)} %param.13) | copy-start | bytes 6148
  18.5 27.2 %copy-start.5 = (f32[512,128]{1,0:T(8,128)S(1)}, f32[512,128]{1,0:T(8,128)}, u32[]{:S(2)}) copy-start(f32[512,128]{1,0:T(8,128)} %param.10) | copy-start | bytes 786436
  18.5 18.4 %all-to-all-start = ((bf16[4,2,512,128]{3,2,1,0:T(8,128)(2,1)}), bf16[4,2,512,128]{3,2,1,0:T(8,128)(2,1)S(1)}, u32[]{:S(2)}, u32[]{:S(2)}) async-start(bf16[4,2,512,128]{3,2,1,0:T(8,128)(2,1)} %bitcast.84), calls=%async_computation | async-start | bytes 2097152 | tf_op jit(solution)/shard_map/all_to_all | solution.py:34
  37.0 8.7 %collective-permute-start.2 = (bf16[512,128]{1,0:T(8,128)(2,1)S(1)}, bf16[512,128]{1,0:T(8,128)(2,1)S(1)}, u32[]{:S(2)}, u32[]{:S(2)}) collective-permute-start(bf16[512,128]{1,0:T(8,128)(2,1)S(1)} %fusion.36), channel_id=1, source_target_pairs={{0,4},{1,5},{2,6},{3,7},{4,0},{5,1},{6,2},{7,3},{8,12},{9,13},{10,... | collective-permute-start | bytes 393224 | tf_op jit(solution)/shard_map/ppermute | solution.py:16
  45.7 21.2 %copy-start.1 = (f32[512,128]{1,0:T(8,128)}, f32[512,128]{1,0:T(8,128)S(1)}, u32[]{:S(2)}) copy-start(f32[512,128]{1,0:T(8,128)S(1)} %fusion.33) | copy-start | bytes 786436
  47.7 19.2 %all-to-all-start.1 = ((bf16[8,256,128]{2,1,0:T(8,128)(2,1)}), bf16[8,256,128]{2,1,0:T(8,128)(2,1)S(1)}, u32[]{:S(2)}, u32[]{:S(2)}) async-start(bf16[8,256,128]{2,1,0:T(8,128)(2,1)} %broadcast_in_dim.16), calls=%async_computation.1 | async-start | bytes 1048576 | tf_op jit(solution)/shard_map/all_to_all | solution.py:34
  66.9 1.9 collective-permute-start.3
  83.3 2.9 %collective-permute-start.4 = (bf16[4096,128]{1,0:T(8,128)(2,1)}, bf16[4096,128]{1,0:T(8,128)(2,1)S(1)}, u32[]{:S(2)}, u32[]{:S(2)}) collective-permute-start(bf16[4096,128]{1,0:T(8,128)(2,1)} %get-tuple-element.5), channel_id=1, source_target_pairs={{0,8},{1,9},{2,10},{3,11},{4,12},{5,13},{6,14},{7,15},{8,0},{9,1},... | collective-permute-start | bytes 3145736 | tf_op jit(solution)/shard_map/ppermute | solution.py:16
  107.0 5.6 %collective-permute-start.5 = (bf16[256,128]{1,0:T(8,128)(2,1)S(1)}, bf16[256,128]{1,0:T(8,128)(2,1)S(1)}, u32[]{:S(2)}, u32[]{:S(2)}) collective-permute-start(bf16[256,128]{1,0:T(8,128)(2,1)S(1)} %fusion.40), channel_id=1, source_target_pairs={{0,4},{1,5},{2,6},{3,7},{4,0},{5,1},{6,2},{7,3},{8,12},{9,13},{10,... | collective-permute-start | bytes 196616 | tf_op jit(solution)/shard_map/ppermute | solution.py:16
  112.6 5.3 %collective-permute-start.6 = (bf16[256,128]{1,0:T(8,128)(2,1)S(1)}, bf16[256,128]{1,0:T(8,128)(2,1)S(1)}, u32[]{:S(2)}, u32[]{:S(2)}) collective-permute-start(bf16[256,128]{1,0:T(8,128)(2,1)S(1)} %fusion.39), channel_id=1, source_target_pairs={{0,4},{1,5},{2,6},{3,7},{4,0},{5,1},{6,2},{7,3},{8,12},{9,13},{10,... | collective-permute-start | bytes 196616 | tf_op jit(solution)/shard_map/ppermute | solution.py:16
  132.9 2.7 %collective-permute-start.7 = (bf16[8,2,256,128]{3,2,0,1:T(8,128)(2,1)S(1)}, bf16[8,2,256,128]{3,2,0,1:T(8,128)(2,1)S(1)}, u32[]{:S(2)}, u32[]{:S(2)}) collective-permute-start(bf16[8,2,256,128]{3,2,0,1:T(8,128)(2,1)S(1)} %copy.24), channel_id=1, source_target_pairs={{0,8},{1,9},{2,10},{3,11},{4,12},{5,13},{6,14},{7,15},{8,0},{9,1},... | collective-permute-start | bytes 3145736 | tf_op jit(solution)/shard_map/ppermute | solution.py:16
  135.8 2.2 slice-start
  136.0 2.7 %slice-start.1 = ((s8[6291456]{0:T(1024)(128)(4,1)}), s8[2097152]{0:T(1024)(128)(4,1)S(1)}, s32[]{:S(2)}) async-start(s8[6291456]{0:T(1024)(128)(4,1)} %bitcast.101), calls=%async_computation.8 | async-start | bytes 4194304
  140.1 6.3 %collective-permute-start.8 = (bf16[256,128]{1,0:T(8,128)(2,1)S(1)}, bf16[256,128]{1,0:T(8,128)(2,1)S(1)}, u32[]{:S(2)}, u32[]{:S(2)}) collective-permute-start(bf16[256,128]{1,0:T(8,128)(2,1)S(1)} %add_convert_fusion.1), channel_id=1, source_target_pairs={{0,4},{1,5},{2,6},{3,7},{4,0},{5,1},{6,2},{7,3},{8,12},{9,13},{10,... | collective-permute-start | bytes 196616 | tf_op jit(solution)/shard_map/ppermute | solution.py:16
  164.9 2.7 %collective-permute-start.9 = (bf16[8,2,256,128]{3,2,0,1:T(8,128)(2,1)S(1)}, bf16[8,2,256,128]{3,2,0,1:T(8,128)(2,1)S(1)}, u32[]{:S(2)}, u32[]{:S(2)}) collective-permute-start(bf16[8,2,256,128]{3,2,0,1:T(8,128)(2,1)S(1)} %copy.31), channel_id=1, source_target_pairs={{0,8},{1,9},{2,10},{3,11},{4,12},{5,13},{6,14},{7,15},{8,0},{9,1},... | collective-permute-start | bytes 3145736 | tf_op jit(solution)/shard_map/ppermute | solution.py:16
  169.7 6.2 %collective-permute-start.10 = (bf16[256,128]{1,0:T(8,128)(2,1)S(1)}, bf16[256,128]{1,0:T(8,128)(2,1)S(1)}, u32[]{:S(2)}, u32[]{:S(2)}) collective-permute-start(bf16[256,128]{1,0:T(8,128)(2,1)S(1)} %get-tuple-element.22), channel_id=1, source_target_pairs={{0,4},{1,5},{2,6},{3,7},{4,0},{5,1},{6,2},{7,3},{8,12},{9,13},{10,... | collective-permute-start | bytes 196616 | tf_op jit(solution)/shard_map/ppermute | solution.py:16
  194.4 2.7 %copy-start.2 = (bf16[8,2,256,128]{3,2,1,0:T(8,128)(2,1)}, bf16[8,2,256,128]{3,2,1,0:T(8,128)(2,1)S(1)}, u32[]{:S(2)}) copy-start(bf16[8,2,256,128]{3,2,1,0:T(8,128)(2,1)S(1)} %all_to_all.38) | copy-start | bytes 3145732
  194.4 2.7 %collective-permute-start.11 = (bf16[8,2,256,128]{3,2,1,0:T(8,128)(2,1)S(1)}, bf16[8,2,256,128]{3,2,1,0:T(8,128)(2,1)S(1)}, u32[]{:S(2)}, u32[]{:S(2)}) collective-permute-start(bf16[8,2,256,128]{3,2,1,0:T(8,128)(2,1)S(1)} %all_to_all.38), channel_id=1, source_target_pairs={{0,8},{1,9},{2,10},{3,11},{4,12},{5,13},{6,14},{7,15},{8,0},{9,1},... | collective-permute-start | bytes 3145736 | tf_op jit(solution)/shard_map/ppermute | solution.py:16
  197.1 1.0 copy-start.4
  227.5 1.9 collective-permute-start.12
  229.6 2.4 %copy-start.3 = (f32[512,128]{1,0:T(8,128)S(1)}, f32[512,128]{1,0:T(8,128)}, u32[]{:S(2)}) copy-start(f32[512,128]{1,0:T(8,128)} %param.9) | copy-start | bytes 786436
